TPU v7x, 32 devices: a whole 2x2x4 slice. The times are simulated.
32 devices in a mesh: comp: 2 (over core), gx: 4 (over y, x), gy: 4 (over z).
Axes of the slice: x: 2, y: 2, z: 4, core: 2. Of those that a mesh axis runs over, the one named last changes fastest.
Arguments:
- state: float32 [2, 8, 96, 3072], P('comp', None, 'gx', 'gy'), may hold values from -6 to 6
- response: float32 [2, 8, 3072], P('comp'), may hold values from -0.95 to 0
- diffusion: float32 [2, 96, 3072], P('comp', 'gx', 'gy'), may hold values from 0.02 to 0.24
- land_mask: int32 [96, 3072], P('gx', 'gy'), may hold values 0 or 1
- couple_src: int32 [2, 4, 4, 16, 128], P('comp', 'gx', 'gy'), may hold values from 0 to 18431
- couple_dst: int32 [2, 4, 4, 16, 128], P('comp', 'gx', 'gy'), may hold values from 0 to 18431
- couple_weight: float32 [2, 4, 4, 16, 128], P('comp', 'gx', 'gy'), may hold values from 0.1 to 1
- couple_count: int32 [2, 4, 4, 16], P('comp', 'gx', 'gy'), may hold values from 0 to 128, as said below
Outputs:
- final_state: float32 [2, 8, 96, 3072], P('comp', None, 'gx', 'gy')
Inputs may be any that keep to these rules, and one draw needn't show every extreme that they name: `couple_count`: at most 128 live slots per ordered device pair; every sending device has one pair with exactly 128.
All inputs are finite; a program needn't handle non-finite values. No bound on the sum of `land_mask` on one device may be relied on, other than what follows from the above.
Results may differ from a plain program's by a relative error of at most 0.0095.
Values may be sent and summed in bfloat16 or wider, within the bound.
A program may use at most 128 MiB of HBM per device.

v0:
```python
import math
import jax
import jax.numpy as jnp
from jax import lax
from jax.sharding import PartitionSpec as P

FC = 4


def extended(block, sides, width):
    for axis, dim in sides:
        count = lax.axis_size(axis)
        forward = [(i, i + 1) for i in range(count - 1)]
        backward = [(target, source) for source, target in forward]
        low = lax.ppermute(
            lax.slice_in_dim(block, block.shape[dim] - width, None, axis=dim), axis, forward
        )
        high = lax.ppermute(lax.slice_in_dim(block, 0, width, axis=dim), axis, backward)
        block = jnp.concatenate([low, block, high], axis=dim)
    return block


def partner(value, axis, stride):
    mask = 2**stride
    pairs = [(source, source ^ mask) for source in range(lax.axis_size(axis))]
    return lax.ppermute(value, axis, pairs)


def make_table(cols):
    split = 64 if cols % 64 == 0 else 1
    wave_idx = jnp.arange(cols // 2, dtype=jnp.int32)[None, :]
    scale = 2.0 * math.pi / cols

    def trig(rows_idx):
        angle = (rows_idx * wave_idx % cols).astype(jnp.float32) * scale
        return (jnp.cos(angle), jnp.sin(angle))

    cos_hi, sin_hi = trig(jnp.arange(cols // split, dtype=jnp.int32)[:, None] * split)
    cos_lo, sin_lo = trig(jnp.arange(split, dtype=jnp.int32)[:, None])
    cos_hi, sin_hi = (cos_hi[:, None], sin_hi[:, None])
    cos_lo, sin_lo = (cos_lo[None], sin_lo[None])
    cos_all = cos_hi * cos_lo - sin_hi * sin_lo
    sin_all = sin_hi * cos_lo + cos_hi * sin_lo
    table = jnp.concatenate([cos_all, sin_all], axis=2).astype(jnp.bfloat16)
    return table.reshape(cols, cols)


def back_transform(filtered, table_part):
    return lax.dot_general(
        filtered, table_part, (((1,), (1,)), ((), ())), preferred_element_type=jnp.float32
    )


def circle_increment(circles, resp_part, table, scale):
    count, rows_part, cols_all = circles.shape
    spec = jnp.dot(circles.reshape(-1, cols_all), table, preferred_element_type=jnp.float32)
    spec = spec.reshape(count, rows_part, cols_all)
    filtered = (spec * resp_part[:, None, :]).astype(jnp.bfloat16)
    incr = (back_transform(filtered.reshape(-1, cols_all), table) * scale).astype(jnp.bfloat16)
    return incr.reshape(count, rows_part, cols_all)


def diffuse(fields, rate):
    padded = extended(fields.astype(jnp.bfloat16), (("gx", 1),), 1).astype(fields.dtype)
    return fields + rate[None] * (padded[:, 2:] + padded[:, :-2] - 2.0 * fields)


def local(
    state, response, diffusion, land_mask, couple_src, couple_dst, couple_weight, couple_count
):
    levels, rows_dev, cols_dev = (state.shape[1], state.shape[2], state.shape[3])
    groups_x = lax.axis_size("gx")
    groups_y = lax.axis_size("gy")
    peers = groups_x * groups_y
    slots = couple_src.shape[4]
    cells = rows_dev * cols_dev
    cols_all = cols_dev * groups_y
    per_level = levels // groups_y
    section = lax.axis_index("comp")
    keep = jnp.where(section == 1, land_mask.astype(jnp.float32), jnp.float32(1.0))
    table = make_table(cols_all)
    scale = 2.0 / cols_all
    src_idx = couple_src.reshape(peers, slots)
    dst_idx = couple_dst.reshape(peers, slots)
    live = jnp.arange(slots, dtype=jnp.int32)[None, :] < couple_count.reshape(peers, 1)
    weights = jnp.where(live, couple_weight.reshape(peers, slots), jnp.float32(0.0))
    first_level = lax.axis_index("gy") * per_level
    resp_mine = lax.dynamic_slice_in_dim(response[0], first_level, per_level, 0)
    rate = diffusion[0]
    fields = state[0]
    surface = fields[:FC].reshape(FC, cells)
    outgoing = jnp.transpose(surface[:, src_idx] * weights[None], (1, 0, 2))
    crossed = partner(outgoing, "comp", 0)
    arrived = lax.all_to_all(crossed, ("gx", "gy"), split_axis=0, concat_axis=0, tiled=True)
    incoming = jnp.transpose(arrived, (1, 0, 2))
    surface = surface.at[:, dst_idx].add(incoming)
    surf = surface.reshape(FC, rows_dev, cols_dev)
    fields = jnp.concatenate([surf, fields[FC:]], axis=0)
    grid_bf = fields.astype(jnp.bfloat16)
    circles = lax.all_to_all(grid_bf, "gy", split_axis=0, concat_axis=2, tiled=True)
    incr = circle_increment(circles, resp_mine, table, scale)
    incr = lax.all_to_all(incr, "gy", split_axis=2, concat_axis=0, tiled=True)
    fields = fields + incr.astype(jnp.float32)
    fields = diffuse(fields, rate) * keep[None]
    return fields[None]


def solution(mesh):
    return jax.shard_map(
        local,
        mesh=mesh,
        in_specs=(
            P("comp", None, "gx", "gy"),
            P("comp", None, None),
            P("comp", "gx", "gy"),
            P("gx", "gy"),
            P("comp", "gx", "gy", None, None),
            P("comp", "gx", "gy", None, None),
            P("comp", "gx", "gy", None, None),
            P("comp", "gx", "gy", None),
        ),
        out_specs=P("comp", None, "gx", "gy"),
        check_vma=False,
    )
```

profile of v0, /device:TPU:4, one launch (start us, length us, event | category | flops | bytes accessed | tf_op | source)
XLA Modules:
  0.0 130.0 jit_solution(9404093053873846128)
XLA Ops:
  0.0 0.0 copy-start
  0.0 0.0 copy-start.5
  0.0 0.0 copy-start.4
  0.0 1.1 fusion.37
  1.2 0.0 copy-start.1
  1.2 5.7 %copy.20 = f32[1,4,24,768]{1,3,2,0:T(8,128)} copy(f32[1,4,24,768]{3,2,1,0:T(8,128)S(1)} %get-tuple-element.7) | data formatting | bytes 589824 | tf_op jit(solution)/shard_map/slice | solution.py:91
  6.9 0.0 copy-done.2
  6.9 9.1 %gather_fusion = f32[2048,4]{1,0:T(8,128)S(1)} fusion(f32[4,18432]{0,1:T(8,128)} %bitcast.57, s32[2048]{0:T(1024)S(1)} %fusion.34), kind=kCustom, calls=%fused_computation | custom fusion | bytes 73728 | tf_op jit(solution)/shard_map/gather | solution.py:92
  16.0 0.3 copy.21
  16.3 0.0 copy-done.3
  16.3 0.0 copy-done.5
  16.4 0.1 bitcast_select_fusion
  16.4 0.1 collective-permute-start
  16.5 1.3 fusion.29
  17.8 1.6 %fusion.21 = (f32[64,1536]{1,0:T(8,128)S(1)}, f32[64,1536]{1,0:T(8,128)S(1)}) fusion(), kind=kLoop, calls=%fused_computation.30 | loop fusion | flops 884736 | bytes 786432 | tf_op jit(solution)/shard_map/sin | solution.py:36
  19.4 0.0 collective-permute-done
  19.4 0.6 copy.22
  20.0 7.3 %all-to-all-start = ((f32[16,4,128]{2,1,0:T(4,128)}), f32[16,4,128]{2,1,0:T(4,128)S(1)}, u32[]{:S(2)}, u32[]{:S(2)}) async-start(f32[16,4,128]{2,1,0:T(4,128)} %copy.22), calls=%async_computation | async-start | bytes 65536 | tf_op jit(solution)/shard_map/all_to_all | solution.py:94
  27.3 0.0 copy-done.4
  27.3 6.1 %all-to-all-done = f32[16,4,128]{2,1,0:T(4,128)S(1)} async-done(((f32[16,4,128]{2,1,0:T(4,128)}), f32[16,4,128]{2,1,0:T(4,128)S(1)}, u32[]{:S(2)}, u32[]{:S(2)}) %all-to-all-start) | async-done | bytes 32800 | tf_op jit(solution)/shard_map/all_to_all | solution.py:94
  33.4 0.4 copy.23
  33.7 17.6 %scatter_fusion = f32[4,18432]{0,1:T(8,128)} fusion(f32[4,18432]{0,1:T(8,128)} %bitcast.58, s32[2048]{0:T(1024)S(1)} %fusion.32, f32[2048,4]{1,0:T(8,128)S(1)} %copy.23), kind=kCustom, calls=%fused_computation.1 | custom fusion | flops 8192 | bytes 106496 | tf_op jit(solution)/shard_map/scatter-add | solution.py:96
  51.4 6.4 %copy.24 = f32[4,24,768]{2,1,0:T(8,128)S(1)} copy(f32[4,24,768]{0,2,1:T(8,128)} %bitcast.59) | data formatting | bytes 589824 | tf_op jit(solution)/shard_map/reshape | solution.py:97
  57.8 0.0 copy-done.1
  57.8 0.7 fusion.16
  58.5 3.6 %all-to-all-start.1 = ((bf16[8,24,768]{2,1,0:T(8,128)(2,1)}), bf16[8,24,768]{2,1,0:T(8,128)(2,1)S(1)}, u32[]{:S(2)}, u32[]{:S(2)}) async-start(bf16[8,24,768]{2,1,0:T(8,128)(2,1)} %fusion.16), calls=%async_computation.1 | async-start | bytes 589824 | tf_op jit(solution)/shard_map/all_to_all | solution.py:100
  62.2 9.6 %subtract_convert_fusion = (bf16[48,64,1536]{2,1,0:T(8,128)(2,1)}, bf16[48,64,1536]{2,1,0:T(8,128)(2,1)}) fusion(f32[64,1536]{1,0:T(8,128)S(1)} %get-tuple-element.13, f32[48,1536]{1,0:T(8,128)S(1)} %get-tuple-element.12, f32[64,1536]{1,0:T(8,128)S(1)} %get-tuple-element.14, f32[48,1536]{1,0:T(8,128)S(1)} %get-tuple-element.11), kind=kLoop, calls=%fused_computation.6 | loop fusion | flops 37748736 | bytes 20250624 | tf_op jit(solution)/shard_map/convert.6
  71.7 0.0 copy-done
  71.7 0.0 all-to-all-done.1
  71.8 0.2 copy.29
  71.9 0.2 dot_general.8
  72.1 8.2 %fusion.7 = bf16[2,24,3072]{2,1,0:T(8,128)(2,1)S(1)} fusion(bf16[2,24,3072]{2,1,0:T(8,128)(2,1)S(1)} %dot_general.8, bf16[3072,1536]{1,0:T(8,128)(2,1)} %bitcast.62, bf16[3072,1536]{1,0:T(8,128)(2,1)} %bitcast.60, f32[2,3072]{1,0:T(2,128)S(1)} %dynamic-slice_bitcast_fusion), kind=kOutput, calls=%fused_computation.10 | convolution fusion | flops 944013312 | bytes 19488768 | tf_op jit(solution)/shard_map/dot_general | solution.py:56
  80.3 9.6 %fusion.10 = bf16[48,3072]{1,0:T(8,128)(2,1)S(1)} fusion(bf16[48,3072]{1,0:T(8,128)(2,1)S(1)} %bitcast.73, bf16[3072,1536]{1,0:T(8,128)(2,1)} %bitcast.63, bf16[3072,1536]{1,0:T(8,128)(2,1)} %bitcast.61), kind=kOutput, calls=%fused_computation.11 | convolution fusion | flops 944013312 | bytes 19464192 | tf_op jit(solution)/shard_map/dot_general | solution.py:49
  90.0 1.9 %copy.26 = bf16[2,24,3072]{1,0,2:T(2,128)(2,1)S(1)} copy(bf16[2,24,3072]{2,1,0:T(8,128)(2,1)S(1)} %bitcast.69) | data formatting | bytes 589824 | tf_op jit(solution)/shard_map/reshape | solution.py:60
  91.9 2.6 %reshape.245 = bf16[4,2,18432]{2,1,0:T(2,128)(2,1)} reshape(bf16[3072,2,24]{2,1,0:T(2,128)(2,1)S(1)} %bitcast.64) | data formatting | bytes 589824
  94.5 4.8 %all-to-all-start.2 = ((bf16[4,2,18432]{2,1,0:T(2,128)(2,1)}), bf16[4,2,18432]{2,1,0:T(2,128)(2,1)S(1)}, u32[]{:S(2)}, u32[]{:S(2)}) async-start(bf16[4,2,18432]{2,1,0:T(2,128)(2,1)} %reshape.245), calls=%async_computation.2 | async-start | bytes 589824 | tf_op jit(solution)/shard_map/all_to_all | solution.py:102
  99.4 8.7 %all-to-all-done.2 = bf16[4,2,18432]{2,1,0:T(2,128)(2,1)S(1)} async-done(((bf16[4,2,18432]{2,1,0:T(2,128)(2,1)}), bf16[4,2,18432]{2,1,0:T(2,128)(2,1)S(1)}, u32[]{:S(2)}, u32[]{:S(2)}) %all-to-all-start.2) | async-done | bytes 294944 | tf_op jit(solution)/shard_map/all_to_all | solution.py:102
  108.1 3.1 %reshape.246 = bf16[3072,2,24]{2,1,0:T(2,128)(2,1)} reshape(bf16[4,2,18432]{2,1,0:T(2,128)(2,1)S(1)} %all-to-all-done.2) | data formatting | bytes 589824
  111.2 2.5 %convert_bitcast_fusion = f32[4,2,24,768]{2,1,3,0:T(2,128)S(1)} fusion(bf16[2,24,4,768]{1,0,3,2:T(2,128)(2,1)} %bitcast.65), kind=kLoop, calls=%fused_computation.12 | loop fusion | flops 147456 | bytes 884736 | tf_op jit(solution)/shard_map/convert_element_type | solution.py:103
  113.7 2.9 %copy.27 = f32[4,2,24,768]{3,2,1,0:T(8,128)} copy(f32[4,2,24,768]{2,1,3,0:T(2,128)S(1)} %convert_bitcast_fusion) | data formatting | bytes 1179648 | tf_op jit(solution)/shard_map/convert_element_type | solution.py:103
  116.5 1.2 fusion.31
  117.8 3.3 %collective-permute-start.2 = (bf16[8,1,768]{2,1,0:T(2,128)(2,1)S(1)}, bf16[8,1,768]{2,1,0:T(2,128)(2,1)S(1)}, u32[]{:S(2)}, u32[]{:S(2)}) collective-permute-start(bf16[8,1,768]{2,1,0:T(2,128)(2,1)S(1)} %get-tuple-element.10), channel_id=1, source_target_pairs={{4,0},{8,4},{12,8},{5,1},{9,5},{13,9},{6,2},{10,6},{14,10},{7,3},{... | collective-permute-start | bytes 36872 | tf_op jit(solution)/shard_map/ppermute | solution.py:18
  121.1 2.5 %collective-permute-start.1 = (bf16[8,1,768]{2,1,0:T(2,128)(2,1)S(1)}, bf16[8,1,768]{2,1,0:T(2,128)(2,1)S(1)}, u32[]{:S(2)}, u32[]{:S(2)}) collective-permute-start(bf16[8,1,768]{2,1,0:T(2,128)(2,1)S(1)} %get-tuple-element.9), channel_id=1, source_target_pairs={{0,4},{4,8},{8,12},{1,5},{5,9},{9,13},{2,6},{6,10},{10,14},{3,7},{... | collective-permute-start | bytes 36872 | tf_op jit(solution)/shard_map/ppermute | solution.py:15
  123.6 0.9 convert_select_fusion
  124.5 0.0 collective-permute-done.2
  124.5 3.2 %collective-permute-done.1 = bf16[8,1,768]{2,1,0:T(2,128)(2,1)S(1)} collective-permute-done((bf16[8,1,768]{2,1,0:T(2,128)(2,1)S(1)}, bf16[8,1,768]{2,1,0:T(2,128)(2,1)S(1)}, u32[]{:S(2)}, u32[]{:S(2)}) %collective-permute-start.1) | collective-permute-done | bytes 12320 | tf_op jit(solution)/shard_map/ppermute | solution.py:15
  127.7 0.1 maximum_convert_fusion
  127.9 2.2 %fusion.15 = f32[1,8,24,768]{3,2,1,0:T(8,128)} fusion(f32[8,26,768]{2,1,0:T(8,128)S(1)} %maximum_convert_fusion, f32[24,768]{1,0:T(8,128)S(1)} %convert_select_fusion, f32[24,768]{1,0:T(8,128)} %bitcast.71, f32[4,2,24,768]{3,2,1,0:T(8,128)} %copy.27, f32[4,24,768]{2,1,0:T(8,128)} %copy-done.1, f32[4,24,768]{2,1,0:T(8,128)S(1)} %copy.24), kind=kLoop, calls=%fused_computation.19 | loop fusion | flops 1179648 | bytes 3096576 | tf_op jit(solution)/shard_map/broadcast_in_dim | solution.py:105
  (8 shorter events, 0.1 us)
Async XLA Ops:
  0.0 71.7 %copy-start = (f32[1,8,3072]{2,1,0:T(8,128)S(1)}, f32[1,8,3072]{2,1,0:T(8,128)}, u32[]{:S(2)}) copy-start(f32[1,8,3072]{2,1,0:T(8,128)} %param.9) | copy-start | bytes 294916
  0.0 6.9 %copy-start.2 = (s32[1,1,1,16,128]{4,3,2,1,0:T(8,128)S(1)}, s32[1,1,1,16,128]{4,3,2,1,0:T(8,128)}, u32[]{:S(2)}) copy-start(s32[1,1,1,16,128]{4,3,2,1,0:T(8,128)} %param.12) | copy-start | bytes 24580
  0.0 16.3 %copy-start.3 = (f32[1,1,1,16,128]{4,3,2,1,0:T(8,128)S(1)}, f32[1,1,1,16,128]{4,3,2,1,0:T(8,128)}, u32[]{:S(2)}) copy-start(f32[1,1,1,16,128]{4,3,2,1,0:T(8,128)} %param.14) | copy-start | bytes 24580
  0.0 16.3 %copy-start.5 = (s32[1,1,1,16]{3,2,1,0:T(1,128)S(1)}, s32[1,1,1,16]{3,2,1,0:T(1,128)}, u32[]{:S(2)}) copy-start(s32[1,1,1,16]{3,2,1,0:T(1,128)} %param.15) | copy-start | bytes 196
  0.0 27.3 %copy-start.4 = (s32[1,1,1,16,128]{4,3,2,1,0:T(8,128)S(1)}, s32[1,1,1,16,128]{4,3,2,1,0:T(8,128)}, u32[]{:S(2)}) copy-start(s32[1,1,1,16,128]{4,3,2,1,0:T(8,128)} %param.13) | copy-start | bytes 24580
  1.2 56.6 %copy-start.1 = (f32[4,24,768]{2,1,0:T(8,128)}, f32[4,24,768]{2,1,0:T(8,128)S(1)}, u32[]{:S(2)}) copy-start(f32[4,24,768]{2,1,0:T(8,128)S(1)} %get-tuple-element.8) | copy-start | bytes 884740
  16.4 2.9 %collective-permute-start = (f32[16,4,128]{2,0,1:T(8,128)S(1)}, f32[16,4,128]{2,0,1:T(8,128)S(1)}, u32[]{:S(2)}, u32[]{:S(2)}) collective-permute-start(f32[16,4,128]{2,0,1:T(8,128)S(1)} %multiply_bitcast_fusion), channel_id=1, source_target_pairs={{0,16},{16,0},{1,17},{17,1},{2,18},{18,2},{3,19},{19,3},{4,20},{20... | collective-permute-start | bytes 98312 | tf_op jit(solution)/shard_map/ppermute | solution.py:26
  20.0 13.4 %all-to-all-start = ((f32[16,4,128]{2,1,0:T(4,128)}), f32[16,4,128]{2,1,0:T(4,128)S(1)}, u32[]{:S(2)}, u32[]{:S(2)}) async-start(f32[16,4,128]{2,1,0:T(4,128)} %copy.22), calls=%async_computation | async-start | bytes 65536 | tf_op jit(solution)/shard_map/all_to_all | solution.py:94
  58.5 13.2 %all-to-all-start.1 = ((bf16[8,24,768]{2,1,0:T(8,128)(2,1)}), bf16[8,24,768]{2,1,0:T(8,128)(2,1)S(1)}, u32[]{:S(2)}, u32[]{:S(2)}) async-start(bf16[8,24,768]{2,1,0:T(8,128)(2,1)} %fusion.16), calls=%async_computation.1 | async-start | bytes 589824 | tf_op jit(solution)/shard_map/all_to_all | solution.py:100
  94.5 13.5 %all-to-all-start.2 = ((bf16[4,2,18432]{2,1,0:T(2,128)(2,1)}), bf16[4,2,18432]{2,1,0:T(2,128)(2,1)S(1)}, u32[]{:S(2)}, u32[]{:S(2)}) async-start(bf16[4,2,18432]{2,1,0:T(2,128)(2,1)} %reshape.245), calls=%async_computation.2 | async-start | bytes 589824 | tf_op jit(solution)/shard_map/all_to_all | solution.py:102
  117.8 6.8 %collective-permute-start.2 = (bf16[8,1,768]{2,1,0:T(2,128)(2,1)S(1)}, bf16[8,1,768]{2,1,0:T(2,128)(2,1)S(1)}, u32[]{:S(2)}, u32[]{:S(2)}) collective-permute-start(bf16[8,1,768]{2,1,0:T(2,128)(2,1)S(1)} %get-tuple-element.10), channel_id=1, source_target_pairs={{4,0},{8,4},{12,8},{5,1},{9,5},{13,9},{6,2},{10,6},{14,10},{7,3},{... | collective-permute-start | bytes 36872 | tf_op jit(solution)/shard_map/ppermute | solution.py:18
  121.1 6.6 %collective-permute-start.1 = (bf16[8,1,768]{2,1,0:T(2,128)(2,1)S(1)}, bf16[8,1,768]{2,1,0:T(2,128)(2,1)S(1)}, u32[]{:S(2)}, u32[]{:S(2)}) collective-permute-start(bf16[8,1,768]{2,1,0:T(2,128)(2,1)S(1)} %get-tuple-element.9), channel_id=1, source_target_pairs={{0,4},{4,8},{8,12},{1,5},{5,9},{9,13},{2,6},{6,10},{10,14},{3,7},{... | collective-permute-start | bytes 36872 | tf_op jit(solution)/shard_map/ppermute | solution.py:15
where the time goes:
time: 131 us; the launch traced here: 130 us
  other arithmetic  37.8 us (29%)
  local copies, waits for them, and re-layouts  34.6 us (26%)
  starting transfers between devices  21.7 us (17%)
  waiting for transfers between devices  17.9 us (14%)
  matrix products  17.8 us (14%)
    scatter-add x1, other arithmetic, local(): surface = surface.at[:, dst_idx].add(incoming)  17.6 us
    dot_general x1, matrix products, back_transform(): lax.dot_general(filtered, table_part, (((1,), (1,)), ((), ())), preferred...  9.63 us
    another operation x1, other arithmetic  9.56 us
    gather x2, local copies, waits for them, and re-layouts, local(): outgoing = jnp.transpose(surface[:, src_idx] * weights[None], (1, 0, 2))  9.47 us
    all_to_all x1, waiting for transfers between devices, local(): incr = lax.all_to_all(incr, 'gy', split_axis=2, concat_axis=0, tiled=True)  8.68 us
    dot_general x1, matrix products, circle_increment(): jnp.dot(circles.reshape(-1, cols_all), table, preferred_element_type=jnp....  8.22 us
    all_to_all x1, starting transfers between devices, local(): lax.all_to_all(crossed, ('gx', 'gy'), split_axis=0, concat_axis=0, tiled=...  7.28 us
    slice x2, local copies, waits for them, and re-layouts, local(): surface = fields[:FC].reshape(FC, cells)  6.81 us
  transfers between devices with their start and end apart: 6, of which 3 were waited for; matrix products, arithmetic and copies ran while one was open for 10% of the time, Pallas kernels for 0%

commit v1 on v0

--- a/solution.py
+++ b/solution.py
@@ -99,7 +99,9 @@
     grid_bf = fields.astype(jnp.bfloat16)
     circles = lax.all_to_all(grid_bf, "gy", split_axis=0, concat_axis=2, tiled=True)
     incr = circle_increment(circles, resp_mine, table, scale)
-    incr = lax.all_to_all(incr, "gy", split_axis=2, concat_axis=0, tiled=True)
+    incr = jnp.concatenate(
+        lax.all_to_all(jnp.stack(jnp.split(incr, lax.axis_size("gy"), axis=2)), "gy", 0, 0), axis=0
+    )
     fields = fields + incr.astype(jnp.float32)
     fields = diffuse(fields, rate) * keep[None]
     return fields[None]

time: 131 us -> 116 us (0.89)
  local copies, waits for them, and re-layouts: 34.6 us -> 24.1 us
  other arithmetic: 37.8 us -> 32.6 us
    unnamed x14, local copies, waits for them, and re-layouts: 5.78 us -> 0.03 us
    convert_element_type x1 -> x0, local copies, waits for them, and re-layouts: 2.86 us -> none  [local(): fields = fields + incr.astype(jnp.float32)]
    convert_element_type x1 -> x0, other arithmetic: 2.49 us -> none  [local(): fields = fields + incr.astype(jnp.float32)]
    reshape x1 -> x0, local copies, waits for them, and re-layouts: 1.89 us -> none  [circle_increment(): return incr.reshape(count, rows_part, cols_all)]
    another operation x1 -> x2, other arithmetic: 9.56 us -> 9.99 us
  transfers between devices with their start and end apart: 6 -> 6, of which waited for: 3 -> 3; matrix products, arithmetic and copies ran while one was open for 10% -> 11% of each run, Pallas kernels for 0% -> 0%
where the time goes in v1:
time: 116 us; the launch traced here: 115 us
  other arithmetic  32.6 us (28%)
  local copies, waits for them, and re-layouts  24.1 us (21%)
  starting transfers between devices  21.7 us (19%)
  waiting for transfers between devices  18.8 us (16%)
  matrix products  17.9 us (15%)
    scatter-add x1, other arithmetic, local(): surface = surface.at[:, dst_idx].add(incoming)  17.6 us
    dot_general x1, matrix products, back_transform(): lax.dot_general(filtered, table_part, (((1,), (1,)), ((), ())), preferred...  9.66 us
    gather x2, local copies, waits for them, and re-layouts, local(): outgoing = jnp.transpose(surface[:, src_idx] * weights[None], (1, 0, 2))  9.47 us
    another operation x1, other arithmetic  9.23 us
    all_to_all x1, waiting for transfers between devices, local(): lax.all_to_all(jnp.stack(jnp.split(incr, lax.axis_size('gy'), axis=2)), '...  8.68 us
    dot_general x1, matrix products, circle_increment(): jnp.dot(circles.reshape(-1, cols_all), table, preferred_element_type=jnp....  8.21 us
    all_to_all x1, starting transfers between devices, local(): lax.all_to_all(crossed, ('gx', 'gy'), split_axis=0, concat_axis=0, tiled=...  7.28 us
    slice x2, local copies, waits for them, and re-layouts, local(): surface = fields[:FC].reshape(FC, cells)  6.8 us
  transfers between devices with their start and end apart: 6, of which 3 were waited for; matrix products, arithmetic and copies ran while one was open for 11% of the time, Pallas kernels for 0%

profile of v1, /device:TPU:4, one launch (start us, length us, event | category | flops | bytes accessed | tf_op | source)
XLA Modules:
  0.0 115.3 jit_solution(15895539600735677836)
XLA Ops:
  0.0 0.0 copy-start
  0.0 0.0 copy-start.3
  0.0 0.0 copy-start.4
  0.0 0.0 copy-start.6
  0.0 0.0 copy-start.5
  0.0 1.1 fusion.37
  1.2 5.7 %copy.17 = f32[1,4,24,768]{1,3,2,0:T(8,128)} copy(f32[1,4,24,768]{3,2,1,0:T(8,128)S(1)} %get-tuple-element.7) | data formatting | bytes 589824 | tf_op jit(solution)/shard_map/slice | solution.py:91
  6.8 0.0 copy-done.3
  6.8 9.1 %gather_fusion = f32[2048,4]{1,0:T(8,128)S(1)} fusion(f32[4,18432]{0,1:T(8,128)} %bitcast.57, s32[2048]{0:T(1024)S(1)} %fusion.34), kind=kCustom, calls=%fused_computation | custom fusion | bytes 73728 | tf_op jit(solution)/shard_map/gather | solution.py:92
  16.0 0.3 copy.18
  16.3 0.0 copy-done.4
  16.3 0.0 copy-done.6
  16.3 0.1 bitcast_select_fusion
  16.4 0.1 collective-permute-start
  16.5 1.3 %fusion.30 = (f32[48,1536]{1,0:T(8,128)S(1)}, f32[48,1536]{1,0:T(8,128)S(1)}) fusion(s32[48]{0:T(128)S(1)} %iota_multiply_fusion), kind=kLoop, calls=%fused_computation.41 | loop fusion | flops 663552 | bytes 590016 | tf_op jit(solution)/shard_map/cos | solution.py:36
  17.8 1.6 %fusion.21 = (f32[64,1536]{1,0:T(8,128)S(1)}, f32[64,1536]{1,0:T(8,128)S(1)}) fusion(), kind=kLoop, calls=%fused_computation.29 | loop fusion | flops 884736 | bytes 786432 | tf_op jit(solution)/shard_map/sin | solution.py:36
  19.4 0.0 collective-permute-done
  19.4 0.6 copy.19
  20.0 7.3 %all-to-all-start = ((f32[16,4,128]{2,1,0:T(4,128)}), f32[16,4,128]{2,1,0:T(4,128)S(1)}, u32[]{:S(2)}, u32[]{:S(2)}) async-start(f32[16,4,128]{2,1,0:T(4,128)} %copy.19), calls=%async_computation | async-start | bytes 65536 | tf_op jit(solution)/shard_map/all_to_all | solution.py:94
  27.3 0.0 copy-done.5
  27.3 6.1 %all-to-all-done = f32[16,4,128]{2,1,0:T(4,128)S(1)} async-done(((f32[16,4,128]{2,1,0:T(4,128)}), f32[16,4,128]{2,1,0:T(4,128)S(1)}, u32[]{:S(2)}, u32[]{:S(2)}) %all-to-all-start) | async-done | bytes 32800 | tf_op jit(solution)/shard_map/all_to_all | solution.py:94
  33.4 0.4 copy.20
  33.7 17.6 %scatter_fusion = f32[4,18432]{0,1:T(8,128)} fusion(f32[4,18432]{0,1:T(8,128)} %bitcast.58, s32[2048]{0:T(1024)S(1)} %fusion.32, f32[2048,4]{1,0:T(8,128)S(1)} %copy.20), kind=kCustom, calls=%fused_computation.1 | custom fusion | flops 8192 | bytes 106496 | tf_op jit(solution)/shard_map/scatter-add | solution.py:96
  51.4 6.4 %copy.21 = f32[4,24,768]{2,1,0:T(8,128)S(1)} copy(f32[4,24,768]{0,2,1:T(8,128)} %bitcast.59) | data formatting | bytes 589824 | tf_op jit(solution)/shard_map/reshape | solution.py:97
  57.8 0.8 fusion.16
  58.5 3.5 %all-to-all-start.1 = ((bf16[8,24,768]{2,1,0:T(8,128)(2,1)}), bf16[8,24,768]{2,1,0:T(8,128)(2,1)S(1)}, u32[]{:S(2)}, u32[]{:S(2)}) async-start(bf16[8,24,768]{2,1,0:T(8,128)(2,1)} %fusion.16), calls=%async_computation.1 | async-start | bytes 589824 | tf_op jit(solution)/shard_map/all_to_all | solution.py:100
  62.0 9.2 %subtract_convert_fusion = (bf16[48,64,1536]{2,1,0:T(8,128)(2,1)}, bf16[48,64,1536]{2,1,0:T(8,128)(2,1)}) fusion(f32[64,1536]{1,0:T(8,128)S(1)} %get-tuple-element.17, f32[48,1536]{1,0:T(8,128)S(1)} %get-tuple-element.16, f32[64,1536]{1,0:T(8,128)S(1)} %get-tuple-element.18, f32[48,1536]{1,0:T(8,128)S(1)} %get-tuple-element.15), kind=kLoop, calls=%fused_computation.6 | loop fusion | flops 37748736 | bytes 20250624 | tf_op jit(solution)/shard_map/convert.4
  71.2 0.0 copy-done
  71.2 0.0 all-to-all-done.1
  71.2 0.2 copy.24
  71.4 0.2 dot_general.8
  71.6 8.2 %fusion.7 = bf16[2,24,3072]{2,1,0:T(8,128)(2,1)S(1)} fusion(bf16[2,24,3072]{2,1,0:T(8,128)(2,1)S(1)} %dot_general.8, bf16[3072,1536]{1,0:T(8,128)(2,1)} %bitcast.62, bf16[3072,1536]{1,0:T(8,128)(2,1)} %bitcast.60, f32[2,3072]{1,0:T(2,128)S(1)} %dynamic-slice_bitcast_fusion), kind=kOutput, calls=%fused_computation.10 | convolution fusion | flops 944013312 | bytes 19488768 | tf_op jit(solution)/shard_map/dot_general | solution.py:56
  79.8 0.0 copy-start.2
  79.8 0.0 copy-start.1
  79.8 9.7 %fusion.10 = bf16[48,3072]{1,0:T(8,128)(2,1)S(1)} fusion(bf16[48,3072]{1,0:T(8,128)(2,1)S(1)} %bitcast.71, bf16[3072,1536]{1,0:T(8,128)(2,1)} %bitcast.63, bf16[3072,1536]{1,0:T(8,128)(2,1)} %bitcast.61), kind=kOutput, calls=%fused_computation.11 | convolution fusion | flops 944013312 | bytes 19464192 | tf_op jit(solution)/shard_map/dot_general | solution.py:49
  89.5 0.8 pad_maximum_fusion.8
  90.3 5.0 %all-to-all-start.2 = ((bf16[4,2,24,768]{3,2,1,0:T(8,128)(2,1)}), bf16[4,2,24,768]{3,2,1,0:T(8,128)(2,1)S(1)}, u32[]{:S(2)}, u32[]{:S(2)}) async-start(bf16[4,2,24,768]{3,2,1,0:T(8,128)(2,1)} %pad_maximum_fusion.8), calls=%async_computation.2 | async-start | bytes 589824 | tf_op jit(solution)/shard_map/all_to_all | solution.py:103
  95.3 8.7 %all-to-all-done.2 = bf16[4,2,24,768]{3,2,1,0:T(8,128)(2,1)S(1)} async-done(((bf16[4,2,24,768]{3,2,1,0:T(8,128)(2,1)}), bf16[4,2,24,768]{3,2,1,0:T(8,128)(2,1)S(1)}, u32[]{:S(2)}, u32[]{:S(2)}) %all-to-all-start.2) | async-done | bytes 294944 | tf_op jit(solution)/shard_map/all_to_all | solution.py:103
  104.0 0.1 fusion.24
  104.1 3.3 %collective-permute-start.2 = (bf16[8,1,768]{2,1,0:T(2,128)(2,1)S(1)}, bf16[8,1,768]{2,1,0:T(2,128)(2,1)S(1)}, u32[]{:S(2)}, u32[]{:S(2)}) collective-permute-start(bf16[8,1,768]{2,1,0:T(2,128)(2,1)S(1)} %get-tuple-element.10), channel_id=1, source_target_pairs={{4,0},{8,4},{12,8},{5,1},{9,5},{13,9},{6,2},{10,6},{14,10},{7,3},{... | collective-permute-start | bytes 36872 | tf_op jit(solution)/shard_map/ppermute | solution.py:18
  107.5 2.5 %collective-permute-start.1 = (bf16[8,1,768]{2,1,0:T(2,128)(2,1)S(1)}, bf16[8,1,768]{2,1,0:T(2,128)(2,1)S(1)}, u32[]{:S(2)}, u32[]{:S(2)}) collective-permute-start(bf16[8,1,768]{2,1,0:T(2,128)(2,1)S(1)} %get-tuple-element.9), channel_id=1, source_target_pairs={{0,4},{4,8},{8,12},{1,5},{5,9},{9,13},{2,6},{6,10},{10,14},{3,7},{... | collective-permute-start | bytes 36872 | tf_op jit(solution)/shard_map/ppermute | solution.py:15
  110.0 0.0 copy-done.2
  110.0 0.0 collective-permute-done.2
  110.0 4.0 %collective-permute-done.1 = bf16[8,1,768]{2,1,0:T(2,128)(2,1)S(1)} collective-permute-done((bf16[8,1,768]{2,1,0:T(2,128)(2,1)S(1)}, bf16[8,1,768]{2,1,0:T(2,128)(2,1)S(1)}, u32[]{:S(2)}, u32[]{:S(2)}) %collective-permute-start.1) | collective-permute-done | bytes 12320 | tf_op jit(solution)/shard_map/ppermute | solution.py:15
  114.1 0.1 maximum_convert_fusion
  114.2 0.0 copy-done.1
  114.2 1.0 fusion.15
  (8 shorter events, 0.1 us)
Async XLA Ops:
  0.0 71.2 %copy-start = (f32[1,8,3072]{2,1,0:T(8,128)S(1)}, f32[1,8,3072]{2,1,0:T(8,128)}, u32[]{:S(2)}) copy-start(f32[1,8,3072]{2,1,0:T(8,128)} %param.9) | copy-start | bytes 294916
  0.0 6.8 %copy-start.3 = (s32[1,1,1,16,128]{4,3,2,1,0:T(8,128)S(1)}, s32[1,1,1,16,128]{4,3,2,1,0:T(8,128)}, u32[]{:S(2)}) copy-start(s32[1,1,1,16,128]{4,3,2,1,0:T(8,128)} %param.12) | copy-start | bytes 24580
  0.0 16.3 %copy-start.4 = (f32[1,1,1,16,128]{4,3,2,1,0:T(8,128)S(1)}, f32[1,1,1,16,128]{4,3,2,1,0:T(8,128)}, u32[]{:S(2)}) copy-start(f32[1,1,1,16,128]{4,3,2,1,0:T(8,128)} %param.14) | copy-start | bytes 24580
  0.0 16.3 %copy-start.6 = (s32[1,1,1,16]{3,2,1,0:T(1,128)S(1)}, s32[1,1,1,16]{3,2,1,0:T(1,128)}, u32[]{:S(2)}) copy-start(s32[1,1,1,16]{3,2,1,0:T(1,128)} %param.15) | copy-start | bytes 196
  0.0 27.3 %copy-start.5 = (s32[1,1,1,16,128]{4,3,2,1,0:T(8,128)S(1)}, s32[1,1,1,16,128]{4,3,2,1,0:T(8,128)}, u32[]{:S(2)}) copy-start(s32[1,1,1,16,128]{4,3,2,1,0:T(8,128)} %param.13) | copy-start | bytes 24580
  16.4 2.9 %collective-permute-start = (f32[16,4,128]{2,0,1:T(8,128)S(1)}, f32[16,4,128]{2,0,1:T(8,128)S(1)}, u32[]{:S(2)}, u32[]{:S(2)}) collective-permute-start(f32[16,4,128]{2,0,1:T(8,128)S(1)} %multiply_bitcast_fusion), channel_id=1, source_target_pairs={{0,16},{16,0},{1,17},{17,1},{2,18},{18,2},{3,19},{19,3},{4,20},{20... | collective-permute-start | bytes 98312 | tf_op jit(solution)/shard_map/ppermute | solution.py:26
  20.0 13.4 %all-to-all-start = ((f32[16,4,128]{2,1,0:T(4,128)}), f32[16,4,128]{2,1,0:T(4,128)S(1)}, u32[]{:S(2)}, u32[]{:S(2)}) async-start(f32[16,4,128]{2,1,0:T(4,128)} %copy.19), calls=%async_computation | async-start | bytes 65536 | tf_op jit(solution)/shard_map/all_to_all | solution.py:94
  58.5 12.7 %all-to-all-start.1 = ((bf16[8,24,768]{2,1,0:T(8,128)(2,1)}), bf16[8,24,768]{2,1,0:T(8,128)(2,1)S(1)}, u32[]{:S(2)}, u32[]{:S(2)}) async-start(bf16[8,24,768]{2,1,0:T(8,128)(2,1)} %fusion.16), calls=%async_computation.1 | async-start | bytes 589824 | tf_op jit(solution)/shard_map/all_to_all | solution.py:100
  79.8 30.2 %copy-start.2 = (s32[24,768]{1,0:T(8,128)S(1)}, s32[24,768]{1,0:T(8,128)}, u32[]{:S(2)}) copy-start(s32[24,768]{1,0:T(8,128)} %param.11) | copy-start | bytes 221188
  79.8 34.4 %copy-start.1 = (f32[1,24,768]{2,1,0:T(8,128)S(1)}, f32[1,24,768]{2,1,0:T(8,128)}, u32[]{:S(2)}) copy-start(f32[1,24,768]{2,1,0:T(8,128)} %param.10) | copy-start | bytes 221188
  90.3 13.7 %all-to-all-start.2 = ((bf16[4,2,24,768]{3,2,1,0:T(8,128)(2,1)}), bf16[4,2,24,768]{3,2,1,0:T(8,128)(2,1)S(1)}, u32[]{:S(2)}, u32[]{:S(2)}) async-start(bf16[4,2,24,768]{3,2,1,0:T(8,128)(2,1)} %pad_maximum_fusion.8), calls=%async_computation.2 | async-start | bytes 589824 | tf_op jit(solution)/shard_map/all_to_all | solution.py:103
  104.1 5.9 %collective-permute-start.2 = (bf16[8,1,768]{2,1,0:T(2,128)(2,1)S(1)}, bf16[8,1,768]{2,1,0:T(2,128)(2,1)S(1)}, u32[]{:S(2)}, u32[]{:S(2)}) collective-permute-start(bf16[8,1,768]{2,1,0:T(2,128)(2,1)S(1)} %get-tuple-element.10), channel_id=1, source_target_pairs={{4,0},{8,4},{12,8},{5,1},{9,5},{13,9},{6,2},{10,6},{14,10},{7,3},{... | collective-permute-start | bytes 36872 | tf_op jit(solution)/shard_map/ppermute | solution.py:18
  107.5 6.6 %collective-permute-start.1 = (bf16[8,1,768]{2,1,0:T(2,128)(2,1)S(1)}, bf16[8,1,768]{2,1,0:T(2,128)(2,1)S(1)}, u32[]{:S(2)}, u32[]{:S(2)}) collective-permute-start(bf16[8,1,768]{2,1,0:T(2,128)(2,1)S(1)} %get-tuple-element.9), channel_id=1, source_target_pairs={{0,4},{4,8},{8,12},{1,5},{5,9},{9,13},{2,6},{6,10},{10,14},{3,7},{... | collective-permute-start | bytes 36872 | tf_op jit(solution)/shard_map/ppermute | solution.py:15
